TPU v7x, 256 devices: a whole 4x4x8 slice. The times are simulated.
256 devices in a mesh: tm: 32 (over y, x, core), space: 8 (over z).
Axes of the slice: x: 4, y: 4, z: 8, core: 2. Of those that a mesh axis runs over, the one named last changes fastest.
Arguments:
- frames_in: bfloat16 [32, 128, 128, 256], P('tm', 'space'), may hold values from -6 to 6
- w_input: bfloat16 [3, 3, 256, 256], replicated, may hold values from -0.125 to 0.125
- decay_rate: float32 [128], replicated, may hold values from 0.001 to 0.2
- phase: float32 [128], replicated, may hold values from -3.140625 to 3.140625
- w_output: bfloat16 [3, 3, 256, 256], replicated, may hold values from -0.125 to 0.125
Outputs:
- frames_out: bfloat16 [32, 128, 128, 256], P('tm', 'space')
All inputs are finite; a program needn't handle non-finite values.
Results may differ from a plain program's by a relative error of at most 0.0029.
Values may be sent and summed in bfloat16 or wider, within the bound.
A program may use at most 192 MiB of HBM per device.

v0:
```python
import jax
import jax.numpy as jnp
from jax import lax
from jax.sharding import PartitionSpec as P


def with_halo(block, sides, width):
    for axis, dim in sides:
        count = lax.axis_size(axis)
        forward = [(i, i + 1) for i in range(count - 1)]
        backward = [(target, source) for source, target in forward]
        low = lax.ppermute(
            lax.slice_in_dim(block, block.shape[dim] - width, None, axis=dim), axis, forward
        )
        high = lax.ppermute(lax.slice_in_dim(block, 0, width, axis=dim), axis, backward)
        block = jnp.concatenate([low, block, high], axis=dim)
    return block


def entering(value, axis, join, neutral):
    count, mine = (lax.axis_size(axis), lax.axis_index(axis))
    pieces = jax.tree.map(lambda part: lax.all_gather(part, axis), value)
    subtotal = jax.tree.map(
        lambda part, zero: jnp.full_like(part, 0) + jnp.asarray(zero, part.dtype), value, neutral
    )

    def turn(position, subtotal):
        longer = join(subtotal, jax.tree.map(lambda part: part[position], pieces))
        return jax.tree.map(lambda new, old: jnp.where(position < mine, new, old), longer, subtotal)

    return lax.fori_loop(0, count - 1, turn, subtotal)


def convolve_rows(padded, kernel):
    return lax.conv_general_dilated(
        padded,
        kernel,
        (1, 1),
        ((0, 0), (1, 1)),
        dimension_numbers=("NHWC", "HWIO", "NHWC"),
        preferred_element_type=jnp.float32,
    )


def local_recurrence(drive, decay_rate, phase):
    states_n = decay_rate.shape[0]
    magnitude = jnp.exp(-decay_rate)
    lam_re = magnitude * jnp.cos(phase)
    lam_im = magnitude * jnp.sin(phase)
    factor = jnp.sqrt(1.0 - magnitude * magnitude)
    feed = drive * jnp.concatenate([factor, factor])

    def advance(carry, item):
        prev_re, prev_im = carry
        new_re = lam_re * prev_re - lam_im * prev_im + item[..., :states_n]
        new_im = lam_re * prev_im + lam_im * prev_re + item[..., states_n:]
        return ((new_re, new_im), (new_re, new_im))

    start = jnp.zeros(feed.shape[1:3] + (states_n,), jnp.float32)
    return lax.scan(advance, (start, start), feed)


def on_device(frames_in, w_input, decay_rate, phase, w_output):
    count = frames_in.shape[0]
    padded = with_halo(frames_in, (("space", 1),), 1)
    drive = convolve_rows(padded, w_input)
    (end_re, end_im), (local_re, local_im) = local_recurrence(drive, decay_rate, phase)
    block_mag = jnp.exp(-decay_rate * count)
    block_re = block_mag * jnp.cos(phase * count)
    block_im = block_mag * jnp.sin(phase * count)

    def combine(earlier, later):
        mult_re = later[0] * earlier[0] - later[1] * earlier[1]
        mult_im = later[0] * earlier[1] + later[1] * earlier[0]
        sum_re = later[0] * earlier[2] - later[1] * earlier[3] + later[2]
        sum_im = later[0] * earlier[3] + later[1] * earlier[2] + later[3]
        return (mult_re, mult_im, sum_re, sum_im)

    identity = (
        jnp.ones_like(block_re),
        jnp.zeros_like(block_im),
        jnp.zeros_like(end_re),
        jnp.zeros_like(end_im),
    )
    scanned = entering((block_re, block_im, end_re, end_im), "tm", combine, identity)
    carry_re, carry_im = (scanned[2], scanned[3])
    steps_ahead = (jnp.arange(count, dtype=jnp.float32) + 1.0)[:, None]
    power_mag = jnp.exp(-decay_rate[None, :] * steps_ahead)
    power_re = (power_mag * jnp.cos(phase[None, :] * steps_ahead))[:, None, None, :]
    power_im = (power_mag * jnp.sin(phase[None, :] * steps_ahead))[:, None, None, :]
    state_re = local_re + power_re * carry_re[None] - power_im * carry_im[None]
    state_im = local_im + power_re * carry_im[None] + power_im * carry_re[None]
    state_b = jnp.concatenate([state_re, state_im], axis=-1).astype(jnp.bfloat16)
    padded_state = with_halo(state_b, (("space", 1),), 1)
    mixed = convolve_rows(padded_state, w_output)
    return (frames_in.astype(jnp.float32) + jax.nn.gelu(mixed, approximate=False)).astype(
        jnp.bfloat16
    )


def solution(mesh):
    in_specs = (P("tm", "space", None, None), P(), P(), P(), P())
    out_specs = P("tm", "space", None, None)
    return jax.shard_map(
        on_device, mesh=mesh, in_specs=in_specs, out_specs=out_specs, check_vma=False
    )
```

profile of v0, /device:TPU:65, one launch (start us, length us, event | category | flops | bytes accessed | tf_op | source)
XLA Modules:
  0.0 416.9 jit_solution(15634686609988875860)
XLA Ops:
  7.5 3.5 collective-permute-start
  11.1 1.9 collective-permute-start.1
  13.8 3.7 collective-permute-done.1
  20.5 2.3 reshape.69
  23.5 3.0 select_multiply_fusion
  29.7 23.7 %all-gather.4 = f32[32,1,128]{2,1,0:T(1,128)S(1)} all-gather(f32[1,1,128]{2,1,0:T(1,128)S(1)} %bitcast.65), channel_id=2, replica_groups=mesh['tm'=32,'space'=8] {'tm'}, dimensions={0}, use_global_device_ids=true | all-gather | bytes 16896 | tf_op jit(solution)/shard_map/all_gather | solution.py:22
  53.5 20.6 %all-gather.5 = f32[32,1,128]{2,1,0:T(1,128)S(1)} all-gather(f32[1,1,128]{2,1,0:T(1,128)S(1)} %bitcast.64), channel_id=3, replica_groups=mesh['tm'=32,'space'=8] {'tm'}, dimensions={0}, use_global_device_ids=true | all-gather | bytes 16896 | tf_op jit(solution)/shard_map/all_gather | solution.py:22
  74.0 87.4 %all-gather.11.cloned.1.call-done = f32[512,128,128]{2,0,1:T(8,128)} async-done(((f32[16,128,128]{2,0,1:T(8,128)}), f32[512,128,128]{2,0,1:T(8,128)}) %all-gather.11.cloned.1.call-update) | async-done | bytes 33554448 | tf_op jit(solution)/shard_map/all_gather | solution.py:22
  161.5 133.3 %all-gather.9.cloned.1.call-done = f32[512,128,128]{2,0,1:T(8,128)} async-done(((f32[16,128,128]{2,0,1:T(8,128)}), f32[512,128,128]{2,0,1:T(8,128)}) %all-gather.9.cloned.1.call-update) | async-done | bytes 33554448 | tf_op jit(solution)/shard_map/all_gather | solution.py:22
  294.8 88.2 %while.10 = (s32[]{:T(128)}, f32[16,128,128]{2,1,0:T(8,128)S(1)}, f32[16,128,128]{2,1,0:T(8,128)S(1)}, s32[]{:T(128)}, f32[32,128]{1,0:T(8,128)S(1)}, /*index=5*...) while((s32[]{:T(128)}, f32[16,128,128]{2,1,0:T(8,128)S(1)}, ...), condition=%wide.region_1.2_spmd.clone, body=%wide.region_0.1_spmd.clone.sunk | while | flops 3145732 | bytes 10488969 | solution.py:31
  294.8 1.8 constant_dynamic-slice_fusion.5
  297.8 1.7 constant_dynamic-slice_fusion.5
  300.6 1.7 constant_dynamic-slice_fusion.5
  303.4 1.7 constant_dynamic-slice_fusion.5
  306.3 1.7 constant_dynamic-slice_fusion.5
  309.1 1.7 constant_dynamic-slice_fusion.5
  314.8 1.7 constant_dynamic-slice_fusion.5
  317.7 1.7 constant_dynamic-slice_fusion.5
  320.5 1.7 constant_dynamic-slice_fusion.5
  383.0 2.5 fusion.34
  385.8 3.2 collective-permute-start.2
  389.0 2.3 collective-permute-start.3
  392.5 4.2 %collective-permute-done.3 = bf16[1,1,128,256]{3,1,2,0:T(2,128)(2,1)S(1)} collective-permute-done((bf16[1,1,128,256]{3,1,2,0:T(2,128)(2,1)S(1)}, bf16[1,1,128,256]{3,1,2,0:T(2,128)(2,1)S(1)}, u32[]{:S(2)}, u32[]{:S(2)}) %collective-permute-start.3) | collective-permute-done | bytes 65568 | tf_op jit(solution)/shard_map/ppermute | solution.py:15
  399.1 7.5 %fusion.9 = f32[16,8,17,256]{3,1,2,0:T(8,128)S(1)} fusion(bf16[3,3,256,256]{3,2,1,0:T(8,128)(2,1)S(1)} %copy-done.4, bf16[18,1,7,2,256]{4,2,3,0,1:T(8,128)(2,1)S(1)} %slice.34, bf16[18,1,8,17,256]{4,2,3,0,1:T(8,128)(2,1)S(1)} %copy.33, pred[8,17]{0,1:T(8,128)(4,1)S(1)} %copy-done.5), kind=kOutput, calls=%fused_computation.17 | convolution fusion | flops 2607325184 | bytes 4790408 | tf_op jit(solution)/shard_map/conv_general_dilated | solution.py:35
  (123 shorter events, 87.4 us)
Async XLA Ops:
  6.5 16.6 %copy-start = (bf16[3,3,256,256]{3,2,1,0:T(8,128)(2,1)S(1)}, bf16[3,3,256,256]{3,2,1,0:T(8,128)(2,1)}, u32[]{:S(2)}) copy-start(bf16[3,3,256,256]{3,2,1,0:T(8,128)(2,1)} %param.8) | copy-start | bytes 3538948
  6.5 155.0 %all-gather.11.cloned.1.call-start = ((), (), s32[]{:S(2)}) async-start(), calls=%async_computation.1 | async-start | bytes 34603008 | tf_op jit(solution)/shard_map/all_gather | solution.py:22
  7.5 6.2 %collective-permute-start = (bf16[1,1,128,256]{3,2,1,0:T(8,128)(2,1)S(1)}, bf16[1,1,128,256]{3,2,1,0:T(8,128)(2,1)S(1)}, u32[]{:S(2)}, u32[]{:S(2)}) collective-permute-start(bf16[1,1,128,256]{3,2,1,0:T(8,128)(2,1)S(1)} %get-tuple-element.245), channel_id=1, source_target_pairs={{0,1},{1,2},{2,3},{3,4},{4,5},{5,6},{6,7},{8,9},{9,10},{10,11},{11... | collective-permute-start | bytes 196616 | tf_op jit(solution)/shard_map/ppermute | solution.py:12
  11.1 6.4 %collective-permute-start.1 = (bf16[1,1,128,256]{3,2,1,0:T(8,128)(2,1)S(1)}, bf16[1,1,128,256]{3,2,1,0:T(8,128)(2,1)S(1)}, u32[]{:S(2)}, u32[]{:S(2)}) collective-permute-start(bf16[1,1,128,256]{3,2,1,0:T(8,128)(2,1)S(1)} %get-tuple-element.246), channel_id=1, source_target_pairs={{1,0},{2,1},{3,2},{4,3},{5,4},{6,5},{7,6},{9,8},{10,9},{11,10},{12... | collective-permute-start | bytes 196616 | tf_op jit(solution)/shard_map/ppermute | solution.py:15
  22.8 0.7 copy-start.5
  29.0 265.9 %all-gather.9.cloned.1.call-start = ((), (), s32[]{:S(2)}) async-start(), calls=%async_computation | async-start | bytes 34603008 | tf_op jit(solution)/shard_map/all_gather | solution.py:22
  294.8 88.2 %copy-start.2 = (f32[16,128,128]{2,0,1:T(8,128)S(1)}, f32[16,128,128]{2,0,1:T(8,128)}, u32[]{:S(2)}) copy-start(f32[16,128,128]{2,0,1:T(8,128)} %get-tuple-element.241) | copy-start | bytes 3145732
  385.8 6.7 %collective-permute-start.2 = (bf16[1,1,128,256]{3,1,2,0:T(2,128)(2,1)S(1)}, bf16[1,1,128,256]{3,1,2,0:T(2,128)(2,1)S(1)}, u32[]{:S(2)}, u32[]{:S(2)}) collective-permute-start(bf16[1,1,128,256]{3,1,2,0:T(2,128)(2,1)S(1)} %get-tuple-element.243), channel_id=1, source_target_pairs={{0,1},{1,2},{2,3},{3,4},{4,5},{5,6},{6,7},{8,9},{9,10},{10,11},{11... | collective-permute-start | bytes 196616 | tf_op jit(solution)/shard_map/ppermute | solution.py:12
  389.0 7.7 %collective-permute-start.3 = (bf16[1,1,128,256]{3,1,2,0:T(2,128)(2,1)S(1)}, bf16[1,1,128,256]{3,1,2,0:T(2,128)(2,1)S(1)}, u32[]{:S(2)}, u32[]{:S(2)}) collective-permute-start(bf16[1,1,128,256]{3,1,2,0:T(2,128)(2,1)S(1)} %get-tuple-element.244), channel_id=1, source_target_pairs={{1,0},{2,1},{3,2},{4,3},{5,4},{6,5},{7,6},{9,8},{10,9},{11,10},{12... | collective-permute-start | bytes 196616 | tf_op jit(solution)/shard_map/ppermute | solution.py:15
  397.9 1.3 copy-start.4
  406.7 1.2 copy-start.3
  407.4 2.6 copy-start.1
Sparse Core Ops, SparseCore 0:
  29.1 132.3 all-gather.10
  164.0 130.8 all-gather.8
where the time goes:
time: 420 us; the launch traced here: 417 us
  waiting for transfers between devices  231 us (55%)
  local copies, waits for them, and re-layouts  63.9 us (15%)
  blocking collectives  44.3 us (11%)
  other arithmetic  41.8 us (10%)
  between operations  13.6 us (3%)
  starting transfers between devices  11 us (3%)
  matrix products  10.6 us (3%)
    all_gather x2, waiting for transfers between devices, entering(): pieces = jax.tree.map(lambda part: lax.all_gather(part, axis), value)  221 us
    dynamic_slice x31, local copies, waits for them, and re-layouts, turn(): longer = join(subtotal, jax.tree.map(lambda part: part[position], pieces))  53.2 us
    all_gather x2, blocking collectives, entering(): pieces = jax.tree.map(lambda part: lax.all_gather(part, axis), value)  44.3 us
    select_n x31, other arithmetic, turn(): jnp.where(position < mine, new, old)  33.6 us
    conv_general_dilated x2, matrix products, convolve_rows(): lax.conv_general_dilated(padded, kernel, (1, 1), ((0, 0), (1, 1)), dimens...  10.6 us
  transfers between devices with their start and end apart: 6, of which 5 were waited for; matrix products, arithmetic and copies ran while one was open for 0% of the time, Pallas kernels for 0%

commit v1 on v0

v1 whole, which is shorter than its diff:
```python
import functools

import jax
import jax.numpy as jnp
from jax import lax
from jax.experimental import pallas as pl
from jax.experimental.pallas import tpu as pltpu
from jax.sharding import PartitionSpec as P

MESH = pl.DeviceIdType.MESH
NC = 4
SCALE = 16384.0
F32 = jnp.float32
BF16 = jnp.bfloat16


def encode(v):
    return ((v * jnp.abs(v)) * (v * v)).astype(BF16)


def decode(code):
    w = code.astype(F32)
    root = jnp.sqrt(jnp.sqrt(jnp.abs(w)))
    return jnp.where(w < 0, -root, root)


def times(a, b):
    return (a[0] * b[0] - a[1] * b[1], a[0] * b[1] + a[1] * b[0])


def plus(a, b):
    return (a[0] + b[0], a[1] + b[1])


def kernel(
    chips, nz,
    x_hbm, w1_hbm, w2_hbm, decay_ref, phase_ref,
    o_hbm,
    xs, w1, w2, halo, taps, f_own, f_par, a_out, a_in, c_out, c_in, st, st_oth, ov,
    ld_sem, o_sem, hx_s, hx_r, f_s, f_r, a_s, a_r, c_s, c_r, s_s, s_r, hs_s, hs_r,
):
    t, z = lax.axis_index("tm"), lax.axis_index("space")
    core = lax.rem(t, 2)
    chip = t // 2
    mate = t + 1 - 2 * core
    per = 256 // chips
    low, high = z > 0, z < nz - 1

    def peer(d):
        return lax.rem(chip + d, chips)

    def remote(src, dst, send, recv, tm, zz):
        return pltpu.make_async_remote_copy(
            src_ref=src, dst_ref=dst, send_sem=send, recv_sem=recv,
            device_id=(tm, zz), device_id_type=MESH,
        )

    barrier = pltpu.get_barrier_semaphore()

    def greet(tm, zz):
        pl.semaphore_signal(barrier, inc=1, device_id=(tm, zz), device_id_type=MESH)

    greet(mate, z)

    @pl.when(low)
    def _():
        greet(t, z - 1)

    @pl.when(high)
    def _():
        greet(t, z + 1)

    @pl.when(jnp.logical_and(low, core == 0))
    def _():
        greet(mate, z - 1)

    @pl.when(jnp.logical_and(high, core == 1))
    def _():
        greet(mate, z + 1)

    @pl.loop(1, chips)
    def _(d):
        greet(2 * peer(d) + core, z)

    load_x = pltpu.make_async_copy(x_hbm, xs, ld_sem.at[0])
    load_1 = pltpu.make_async_copy(w1_hbm, w1, ld_sem.at[1])
    load_2 = pltpu.make_async_copy(w2_hbm, w2, ld_sem.at[2])
    load_x.start()
    load_1.start()
    load_2.start()

    decay, phase = decay_ref[...], phase_ref[...]
    mag = jnp.exp(-decay)
    lam = (mag * jnp.cos(phase), mag * jnp.sin(phase))
    lam2 = times(lam, lam)
    factor = jnp.sqrt(1.0 - mag * mag) * SCALE
    factor = jnp.concatenate([factor, factor], axis=1)

    def base(half, i):
        return jnp.where(half == 0, 6 - 2 * i, 8 + 2 * i)

    def spread(row, slot):
        v = row.astype(F32)
        at = lax.broadcasted_iota(jnp.int32, v.shape, 0)
        left = jnp.where(at == 0, 0.0, pltpu.roll(v, 1, 0))
        right = jnp.where(at == 127, 0.0, pltpu.roll(v, 127, 0))
        taps[slot, :, 0:256] = left.astype(BF16)
        taps[slot, :, 256:512] = row
        taps[slot, :, 512:768] = right.astype(BF16)

    def conv(w, row):
        acc = None
        for dy in range(3):
            part = jnp.dot(
                taps[pl.ds(row + dy, 2)].reshape(256, 768), w[dy],
                preferred_element_type=F32,
            )
            acc = part if acc is None else acc + part
        return acc

    def drive(i):
        @pl.loop(0, 2)
        def _(n):
            row = base(jnp.where(n == 0, 1 - core, core), i)
            f_own[pl.ds(row, 2)] = (conv(w1, row) * factor).reshape(2, 128, 256)

    def feed_copy(i):
        rows = pl.ds(base(1 - core, i), 2)
        return remote(f_own.at[rows], f_par.at[i], f_s.at[i], f_r.at[i], mate, z)

    def a_copy(i, d):
        j = peer(d)
        return remote(
            a_out.at[i, pl.ds(pl.multiple_of(j * per, per), per)], a_in.at[i, chip],
            a_s.at[i, j], a_r.at[i, chip], 2 * j + core, z,
        )

    def a_landed(i, d):
        j = peer(d)
        return remote(a_in.at[i, j], a_in.at[i, j], a_s.at[i, j], a_r.at[i, j], 2 * j + core, z)

    def c_copy(i, d):
        j = peer(d)
        return remote(
            c_out.at[i, j], c_in.at[i, pl.ds(pl.multiple_of(chip * per, per), per)],
            c_s.at[i, j], c_r.at[i, chip], 2 * j + core, z,
        )

    def c_landed(i, d):
        j = peer(d)
        there = c_in.at[i, pl.ds(pl.multiple_of(j * per, per), per)]
        return remote(there, there, c_s.at[i, j], c_r.at[i, j], 2 * j + core, z)

    def both_feeds(i, row, r, sub):
        mine = f_own[row + r, sub]
        other = f_par[i, r, sub]
        first = jnp.where(core == 0, mine, other)
        second = jnp.where(core == 0, other, mine)
        return (first[:, :128], first[:, 128:]), (second[:, :128], second[:, 128:])

    def aggregate(i):
        feed_copy(i).wait_recv()
        row = base(core, i)

        @pl.loop(0, 4)
        def _(n):
            r, q = n // 2, lax.rem(n, 2)
            sub = pl.ds(pl.multiple_of(q * 64, 64), 64)
            first, second = both_feeds(i, row, r, sub)
            total = plus(times(lam, first), second)
            out = pl.ds(pl.multiple_of(n * 64, 64), 64)
            a_out[i, out, 0:128] = encode(total[0])
            a_out[i, out, 128:256] = encode(total[1])

        @pl.loop(1, chips)
        def _(d):
            a_copy(i, d).start()

        a_in[i, chip] = a_out[i, pl.ds(pl.multiple_of(chip * per, per), per)]

    def scan(i):
        @pl.loop(1, chips)
        def _(d):
            a_landed(i, d).wait_recv()

        carry = (jnp.zeros((per, 128), F32), jnp.zeros((per, 128), F32))
        for k in range(chips):
            c_out[i, k, :, 0:128] = encode(carry[0])
            c_out[i, k, :, 128:256] = encode(carry[1])
            if k < chips - 1:
                got = (decode(a_in[i, k, :, 0:128]), decode(a_in[i, k, :, 128:256]))
                carry = plus(times(lam2, carry), got)

        @pl.loop(1, chips)
        def _(d):
            c_copy(i, d).start()

        c_in[i, pl.ds(pl.multiple_of(chip * per, per), per)] = c_out[i, chip]

    def mate_copy(i):
        rows = pl.ds(1 + base(core, i), 2)
        return remote(st_oth.at[i], st.at[rows], s_s.at[i], s_r.at[i], mate, z)

    def mate_landed(i):
        rows = pl.ds(1 + base(1 - core, i), 2)
        return remote(st.at[rows], st.at[rows], s_s.at[i], s_r.at[i], mate, z)

    def states(i):
        @pl.loop(1, chips)
        def _(d):
            c_landed(i, d).wait_recv()

        row = base(core, i)

        @pl.loop(0, 4)
        def _(n):
            r, q = n // 2, lax.rem(n, 2)
            sub = pl.ds(pl.multiple_of(q * 64, 64), 64)
            first, second = both_feeds(i, row, r, sub)
            took = pl.ds(pl.multiple_of(n * 64, 64), 64)
            carry = (decode(c_in[i, took, 0:128]), decode(c_in[i, took, 128:256]))
            s0 = plus(times(lam, carry), first)
            s1 = plus(times(lam, s0), second)
            for p in range(2):
                lanes = slice(128 * p, 128 * p + 128)
                own = jnp.where(core == 0, s0[p], s1[p]) * (1.0 / SCALE)
                oth = jnp.where(core == 0, s1[p], s0[p]) * (1.0 / SCALE)
                st[1 + row + r, sub, lanes] = own.astype(BF16)
                st_oth[i, r, sub, lanes] = oth.astype(BF16)

        mate_copy(i).start()

    def spread_states(half, i):
        row = base(half, i)

        @pl.loop(0, 2)
        def _(r):
            spread(st[1 + row + r], 1 + row + r)

    def out_copy(half, i):
        rows = pl.ds(base(half, i), 2)
        return pltpu.make_async_copy(ov.at[rows], o_hbm.at[rows], o_sem.at[half, i])

    def finish(i):
        @pl.loop(0, 2)
        def _(half):
            row = base(half, i)
            mixed = conv(w2, row).reshape(2, 128, 256)
            gelu = 0.5 * mixed * (1.0 + lax.erf(mixed * (0.5 ** 0.5)))
            ov[pl.ds(row, 2)] = (xs[pl.ds(row, 2)].astype(F32) + gelu).astype(BF16)
            out_copy(half, i).start()

    load_x.wait()

    @pl.loop(0, 16)
    def _(r):
        spread(xs[r], 1 + r)

    load_1.wait()
    drive(0)

    pl.semaphore_wait(
        barrier,
        chips + low.astype(jnp.int32) + high.astype(jnp.int32)
        + jnp.where(core == 0, low.astype(jnp.int32), high.astype(jnp.int32)),
    )

    up = remote(xs.at[0], halo.at[1], hx_s.at[0], hx_r.at[1], t, z - 1)
    down = remote(xs.at[15], halo.at[0], hx_s.at[1], hx_r.at[0], t, z + 1)
    from_up = remote(halo.at[0], halo.at[0], hx_s.at[1], hx_r.at[0], t, z - 1)
    from_down = remote(halo.at[1], halo.at[1], hx_s.at[0], hx_r.at[1], t, z + 1)

    feed_copy(0).start()

    @pl.when(low)
    def _():
        up.start()

    @pl.when(high)
    def _():
        down.start()

    @pl.loop(1, NC - 1)
    def _(i):
        drive(i)
        feed_copy(i).start()
        aggregate(i - 1)

    def edges(first, second):
        @pl.when(low)
        def _():
            first()

        @pl.when(jnp.logical_not(low))
        def _():
            taps[0] = jnp.zeros((128, 768), BF16)

        @pl.when(high)
        def _():
            second()

        @pl.when(jnp.logical_not(high))
        def _():
            taps[17] = jnp.zeros((128, 768), BF16)

    def halo_first():
        from_up.wait_recv()
        spread(halo[0], 0)

    def halo_second():
        from_down.wait_recv()
        spread(halo[1], 17)

    edges(halo_first, halo_second)
    drive(NC - 1)
    feed_copy(NC - 1).start()
    aggregate(NC - 2)
    aggregate(NC - 1)

    @pl.loop(0, NC)
    def _(i):
        scan(i)

    last = NC - 1
    own_up = remote(st.at[1], st.at[17], hs_s.at[0], hs_r.at[1], t, z - 1)
    oth_up = remote(st_oth.at[last, 0], st.at[17], hs_s.at[1], hs_r.at[1], mate, z - 1)
    own_down = remote(st.at[16], st.at[0], hs_s.at[0], hs_r.at[0], t, z + 1)
    oth_down = remote(st_oth.at[last, 1], st.at[0], hs_s.at[1], hs_r.at[0], mate, z + 1)
    state_up = remote(st.at[0], st.at[0], hs_s.at[0], hs_r.at[0], t, z - 1)
    state_down = remote(st.at[17], st.at[17], hs_s.at[0], hs_r.at[1], t, z + 1)
    sends_up = jnp.logical_and(core == 0, low)
    sends_down = jnp.logical_and(core == 1, high)

    load_2.wait()
    states(0)
    spread_states(core, 0)
    states(1)
    spread_states(core, 1)
    mate_landed(0).wait_recv()
    spread_states(1 - core, 0)
    states(2)
    spread_states(core, 2)
    mate_landed(1).wait_recv()
    spread_states(1 - core, 1)
    finish(0)
    states(3)

    @pl.when(sends_up)
    def _():
        own_up.start()
        oth_up.start()

    @pl.when(sends_down)
    def _():
        own_down.start()
        oth_down.start()

    spread_states(core, 3)
    mate_landed(2).wait_recv()
    spread_states(1 - core, 2)
    finish(1)
    mate_landed(3).wait_recv()
    spread_states(1 - core, 3)
    finish(2)

    def state_first():
        state_up.wait_recv()
        spread(st[0], 0)

    def state_second():
        state_down.wait_recv()
        spread(st[17], 17)

    edges(state_first, state_second)
    finish(3)

    @pl.when(low)
    def _():
        up.wait_send()

    @pl.when(high)
    def _():
        down.wait_send()

    @pl.when(sends_up)
    def _():
        own_up.wait_send()
        oth_up.wait_send()

    @pl.when(sends_down)
    def _():
        own_down.wait_send()
        oth_down.wait_send()

    @pl.loop(0, NC)
    def _(i):
        feed_copy(i).wait_send()
        mate_copy(i).wait_send()

        @pl.loop(1, chips)
        def _(d):
            a_copy(i, d).wait_send()
            c_copy(i, d).wait_send()

        out_copy(0, i).wait()
        out_copy(1, i).wait()


def solution(mesh):
    chips, nz = mesh.shape["tm"] // 2, mesh.shape["space"]
    per = 256 // chips
    any_spec = pl.BlockSpec(memory_space=pl.ANY)
    vmem_spec = pl.BlockSpec(memory_space=pltpu.VMEM)
    dma = pltpu.SemaphoreType.DMA

    def on_device(frames_in, w_input, decay_rate, phase, w_output):
        out = pl.pallas_call(
            functools.partial(kernel, chips, nz),
            out_shape=jax.ShapeDtypeStruct((16, 128, 256), BF16),
            in_specs=[any_spec, any_spec, any_spec, vmem_spec, vmem_spec],
            out_specs=any_spec,
            scratch_shapes=[
                pltpu.VMEM((16, 128, 256), BF16),
                pltpu.VMEM((3, 768, 256), BF16),
                pltpu.VMEM((3, 768, 256), BF16),
                pltpu.VMEM((2, 128, 256), BF16),
                pltpu.VMEM((18, 128, 768), BF16),
                pltpu.VMEM((16, 128, 256), F32),
                pltpu.VMEM((NC, 2, 128, 256), F32),
                pltpu.VMEM((NC, 256, 256), BF16),
                pltpu.VMEM((NC, chips, per, 256), BF16),
                pltpu.VMEM((NC, chips, per, 256), BF16),
                pltpu.VMEM((NC, 256, 256), BF16),
                pltpu.VMEM((18, 128, 256), BF16),
                pltpu.VMEM((NC, 2, 128, 256), BF16),
                pltpu.VMEM((16, 128, 256), BF16),
                dma((3,)), dma((2, NC)), dma((2,)), dma((2,)), dma((NC,)), dma((NC,)),
                dma((NC, chips)), dma((NC, chips)), dma((NC, chips)), dma((NC, chips)),
                dma((NC,)), dma((NC,)), dma((2,)), dma((2,)),
            ],
            compiler_params=pltpu.CompilerParams(
                collective_id=0, has_side_effects=True, vmem_limit_bytes=48 * 1024 * 1024
            ),
            name="convs5",
        )(
            frames_in[0], w_input.reshape(3, 768, 256), w_output.reshape(3, 768, 256),
            decay_rate.reshape(1, 128), phase.reshape(1, 128),
        )
        return out[None]

    in_specs = (P("tm", "space", None, None), P(), P(), P(), P())
    return jax.shard_map(
        on_device, mesh=mesh, in_specs=in_specs,
        out_specs=P("tm", "space", None, None), check_vma=False,
    )
```

time: 420 us -> 40.6 us (0.10)
  waiting for transfers between devices: 231 us -> 0 us
  local copies, waits for them, and re-layouts: 63.9 us -> 6.05 us
  blocking collectives: 44.3 us -> 0 us
  other arithmetic: 41.8 us -> 0 us
  Pallas kernels: 0 us -> 34.3 us
  between operations: 13.6 us -> 0.01 us
  starting transfers between devices: 11 us -> 0 us
  matrix products: 10.6 us -> 0 us
    all_gather x2 -> x0, waiting for transfers between devices: 221 us -> none  [entering(): pieces = jax.tree.map(lambda part: lax.all_gather(part, axis), value)]
    dynamic_slice x31 -> x0, local copies, waits for them, and re-layouts: 53.2 us -> none  [turn(): longer = join(subtotal, jax.tree.map(lambda part: part[position], pieces))]
    all_gather x2 -> x0, blocking collectives: 44.3 us -> none  [entering(): pieces = jax.tree.map(lambda part: lax.all_gather(part, axis), value)]
    pallas_call x0 -> x1, Pallas kernels: none -> 34.3 us  [on_device(): pl.pallas_call(functools.partial(kernel, chips, nz), out_shape=jax.ShapeD...]
    select_n x31 -> x0, other arithmetic: 33.6 us -> none  [turn(): jnp.where(position < mine, new, old)]
    ppermute x4 -> x0, starting transfers between devices: 10.9 us -> none  [the longest x2 6.73 us: with_halo(): lax.ppermute(lax.slice_in_dim(block, block.shape[dim] - width, None, axis...]
    conv_general_dilated x2 -> x0, matrix products: 10.6 us -> none  [convolve_rows(): lax.conv_general_dilated(padded, kernel, (1, 1), ((0, 0), (1, 1)), dimens...]
    ppermute x4 -> x0, waiting for transfers between devices: 9.15 us -> none  [the longest x2 7.94 us: with_halo(): lax.ppermute(lax.slice_in_dim(block, 0, width, axis=dim), axis, backward)]
  transfers between devices with their start and end apart: 6 -> 0, of which waited for: 5 -> 0; matrix products, arithmetic and copies ran while one was open for 0% -> 0% of each run, Pallas kernels for 0% -> 0%
where the time goes in v1:
time: 40.6 us; the launch traced here: 40.4 us
  Pallas kernels  34.3 us (84%)
  local copies, waits for them, and re-layouts  6.05 us (15%)
    pallas_call x1, Pallas kernels, on_device(): pl.pallas_call(functools.partial(kernel, chips, nz), out_shape=jax.ShapeD...  34.3 us
    unnamed x11, local copies, waits for them, and re-layouts  6.05 us

profile of v1, /device:TPU:65, one launch (start us, length us, event | category | flops | bytes accessed | tf_op | source)
XLA Modules:
  0.0 40.4 jit_solution(212409053053446321)
XLA Ops:
  0.0 0.0 copy-start
  0.0 1.3 %copy-done = bf16[3,3,256,256]{3,2,1,0:T(8,128)(2,1)S(1)} copy-done((bf16[3,3,256,256]{3,2,1,0:T(8,128)(2,1)S(1)}, bf16[3,3,256,256]{3,2,1,0:T(8,128)(2,1)}, u32[]{:S(2)}) %copy-start) | copy-done | bytes 1179672
  1.3 0.0 copy-start.1
  1.3 1.3 %copy-done.1 = bf16[3,3,256,256]{3,2,1,0:T(8,128)(2,1)S(1)} copy-done((bf16[3,3,256,256]{3,2,1,0:T(8,128)(2,1)S(1)}, bf16[3,3,256,256]{3,2,1,0:T(8,128)(2,1)}, u32[]{:S(2)}) %copy-start.1) | copy-done | bytes 1179672
  2.5 0.0 copy-start.2
  2.5 1.2 %copy-done.2 = bf16[1,16,128,256]{3,2,1,0:T(8,128)(2,1)S(1)} copy-done((bf16[1,16,128,256]{3,2,1,0:T(8,128)(2,1)S(1)}, bf16[1,16,128,256]{3,2,1,0:T(8,128)(2,1)}, u32[]{:S(2)}) %copy-start.2) | copy-done | bytes 1048600
  3.8 0.0 copy-start.3
  3.8 0.7 %copy-done.3 = f32[128]{0:T(128)S(1)} copy-done((f32[128]{0:T(128)S(1)}, f32[128]{0:T(128)}, u32[]{:S(2)}) %copy-start.3) | copy-done | bytes 536
  4.4 0.0 copy-start.4
  4.4 0.7 %copy-done.4 = f32[128]{0:T(128)S(1)} copy-done((f32[128]{0:T(128)S(1)}, f32[128]{0:T(128)}, u32[]{:S(2)}) %copy-start.4) | copy-done | bytes 536
  5.1 34.3 %convs5.1 = bf16[16,128,256]{2,1,0:T(8,128)(2,1)S(1)} custom-call(bf16[16,128,256]{2,1,0:T(8,128)(2,1)S(1)} %bitcast.9, bf16[3,768,256]{2,1,0:T(8,128)(2,1)S(1)} %bitcast.7, bf16[3,768,256]{2,1,0:T(8,128)(2,1)S(1)} %bitcast.8, f32[1,128]{1,0:T(1,128)S(1)} %bitcast.10, f32[1,128]{1,0:T(1,128)S(1)} %bitcast.11), custom_call_target="tpu_custom_call" | custom-call | tf_op jit(solution)/shard_map/convs5/pallas_call | solution.py:417
  39.4 1.0 %copy.7 = bf16[1,16,128,256]{3,2,1,0:T(8,128)(2,1)} copy(bf16[1,16,128,256]{3,2,1,0:T(8,128)(2,1)S(1)} %bitcast.6) | data formatting | bytes 2097152
Async XLA Ops:
  0.0 1.3 %copy-start = (bf16[3,3,256,256]{3,2,1,0:T(8,128)(2,1)S(1)}, bf16[3,3,256,256]{3,2,1,0:T(8,128)(2,1)}, u32[]{:S(2)}) copy-start(bf16[3,3,256,256]{3,2,1,0:T(8,128)(2,1)} %param.6) | copy-start | bytes 3538948
  1.3 1.3 %copy-start.1 = (bf16[3,3,256,256]{3,2,1,0:T(8,128)(2,1)S(1)}, bf16[3,3,256,256]{3,2,1,0:T(8,128)(2,1)}, u32[]{:S(2)}) copy-start(bf16[3,3,256,256]{3,2,1,0:T(8,128)(2,1)} %param.9) | copy-start | bytes 3538948
  2.5 1.2 %copy-start.2 = (bf16[1,16,128,256]{3,2,1,0:T(8,128)(2,1)S(1)}, bf16[1,16,128,256]{3,2,1,0:T(8,128)(2,1)}, u32[]{:S(2)}) copy-start(bf16[1,16,128,256]{3,2,1,0:T(8,128)(2,1)} %param.5) | copy-start | bytes 3145732
  3.8 0.7 %copy-start.3 = (f32[128]{0:T(128)S(1)}, f32[128]{0:T(128)}, u32[]{:S(2)}) copy-start(f32[128]{0:T(128)} %param.7) | copy-start | bytes 1540
  4.4 0.7 %copy-start.4 = (f32[128]{0:T(128)S(1)}, f32[128]{0:T(128)}, u32[]{:S(2)}) copy-start(f32[128]{0:T(128)} %param.8) | copy-start | bytes 1540

commit v2 on v1

v2 whole, which is shorter than its diff:
```python
import functools

import jax
import jax.numpy as jnp
from jax import lax
from jax.experimental import pallas as pl
from jax.experimental.pallas import tpu as pltpu
from jax.sharding import PartitionSpec as P

MESH = pl.DeviceIdType.MESH
NC = 4
SCALE = 16384.0
F32 = jnp.float32
BF16 = jnp.bfloat16


def encode(v):
    return ((v * jnp.abs(v)) * (v * v)).astype(BF16)


def decode(code):
    w = code.astype(F32)
    root = jnp.sqrt(jnp.sqrt(jnp.abs(w)))
    return jnp.where(w < 0, -root, root)


def times(a, b):
    return (a[0] * b[0] - a[1] * b[1], a[0] * b[1] + a[1] * b[0])


def plus(a, b):
    return (a[0] + b[0], a[1] + b[1])


def kernel(
    chips, nz,
    x_hbm, w1_hbm, w2_hbm, decay_hbm, phase_hbm,
    ov,
    xs, w1, w2, rates, halo, taps, f_own, f_par, a_out, a_in, c_out, c_in, st, st_oth,
    ld_sem, hx_s, hx_r, f_s, f_r, a_s, a_r, c_s, c_r, s_s, s_r, hs_s, hs_r,
):
    t, z = lax.axis_index("tm"), lax.axis_index("space")
    core = lax.rem(t, 2)
    chip = t // 2
    mate = t + 1 - 2 * core
    per = 256 // chips
    low, high = z > 0, z < nz - 1

    ny, nx = (4, chips // 4) if chips >= 16 else (1, chips)
    offsets = sorted(
        ((dy, dx) for dy in range(ny) for dx in range(nx) if dy or dx),
        key=lambda o: -(min(o[0], ny - o[0]) + min(o[1], nx - o[1])),
    )

    def peer(o):
        return lax.rem(chip // nx + o[0], ny) * nx + lax.rem(lax.rem(chip, nx) + o[1], nx)

    def remote(src, dst, send, recv, tm, zz):
        return pltpu.make_async_remote_copy(
            src_ref=src, dst_ref=dst, send_sem=send, recv_sem=recv,
            device_id=(tm, zz), device_id_type=MESH,
        )

    barrier = pltpu.get_barrier_semaphore()

    def greet(tm, zz):
        pl.semaphore_signal(barrier, inc=1, device_id=(tm, zz), device_id_type=MESH)

    greet(mate, z)

    @pl.when(low)
    def _():
        greet(t, z - 1)

    @pl.when(high)
    def _():
        greet(t, z + 1)

    @pl.when(jnp.logical_and(low, core == 0))
    def _():
        greet(mate, z - 1)

    @pl.when(jnp.logical_and(high, core == 1))
    def _():
        greet(mate, z + 1)

    for o in offsets:
        greet(2 * peer(o) + core, z)

    load_x = pltpu.make_async_copy(x_hbm, xs, ld_sem.at[0])
    load_1 = pltpu.make_async_copy(w1_hbm, w1, ld_sem.at[1])
    load_2 = pltpu.make_async_copy(w2_hbm, w2, ld_sem.at[2])
    load_d = pltpu.make_async_copy(decay_hbm, rates.at[0], ld_sem.at[3])
    load_p = pltpu.make_async_copy(phase_hbm, rates.at[1], ld_sem.at[4])
    load_x.start()
    load_d.start()
    load_p.start()
    load_1.start()
    load_2.start()

    load_d.wait()
    load_p.wait()
    decay, phase = rates[0], rates[1]
    mag = jnp.exp(-decay)
    lam = (mag * jnp.cos(phase), mag * jnp.sin(phase))
    lam2 = times(lam, lam)
    factor = jnp.sqrt(1.0 - mag * mag) * SCALE
    factor = jnp.concatenate([factor, factor], axis=1)

    def base(half, i):
        pair = jnp.where(i == 3, 3, lax.rem(i + 1, 3))
        return jnp.where(half == 0, 2 * pair, 14 - 2 * pair)

    def spread(row, slot):
        v = row.astype(F32)
        at = lax.broadcasted_iota(jnp.int32, v.shape, 0)
        left = jnp.where(at == 0, 0.0, pltpu.roll(v, 1, 0))
        right = jnp.where(at == 127, 0.0, pltpu.roll(v, 127, 0))
        taps[slot, :, 0:256] = left.astype(BF16)
        taps[slot, :, 256:512] = row
        taps[slot, :, 512:768] = right.astype(BF16)

    def conv(w, row, other=None):
        acc = None
        for dy in range(3):
            if other is None:
                seen = taps[pl.ds(row + dy, 2)].reshape(256, 768)
            else:
                seen = jnp.concatenate([taps[row + dy], taps[other + dy]], axis=0)
            part = jnp.dot(seen, w[dy], preferred_element_type=F32)
            acc = part if acc is None else acc + part
        return acc

    def drive(i, between):
        @pl.loop(0, 2)
        def _(n):
            row = base(jnp.where(n == 0, 1 - core, core), i)
            f_own[pl.ds(row, 2)] = (conv(w1, row) * factor).reshape(2, 128, 256)

            @pl.when(n == 0)
            def _():
                between()
                feed_copy(i).start()

    def feed_copy(i):
        rows = pl.ds(base(1 - core, i), 2)
        return remote(f_own.at[rows], f_par.at[i], f_s.at[i], f_r.at[i], mate, z)

    def a_copy(i, d):
        j = peer(d)
        return remote(
            a_out.at[i, pl.ds(pl.multiple_of(j * per, per), per)], a_in.at[i, chip],
            a_s.at[i], a_r.at[i], 2 * j + core, z,
        )

    def a_all(i):
        blocks = a_in.at[i, pl.ds(0, chips - 1)]
        return remote(blocks, blocks, a_s.at[i], a_r.at[i], mate, z)

    def c_copy(i, d):
        j = peer(d)
        return remote(
            c_out.at[i, j], c_in.at[i, pl.ds(pl.multiple_of(chip * per, per), per)],
            c_s.at[i], c_r.at[i], 2 * j + core, z,
        )

    def c_all(i):
        blocks = c_in.at[i, pl.ds(0, (chips - 1) * per)]
        return remote(blocks, blocks, c_s.at[i], c_r.at[i], mate, z)

    def both_feeds(i, row, r, sub):
        mine = f_own[row + r, sub]
        other = f_par[i, r, sub]
        first = jnp.where(core == 0, mine, other)
        second = jnp.where(core == 0, other, mine)
        return (first[:, :128], first[:, 128:]), (second[:, :128], second[:, 128:])

    def aggregate(i):
        feed_copy(i).wait_recv()
        row = base(core, i)

        @pl.loop(0, 4)
        def _(n):
            r, q = n // 2, lax.rem(n, 2)
            sub = pl.ds(pl.multiple_of(q * 64, 64), 64)
            first, second = both_feeds(i, row, r, sub)
            total = plus(times(lam, first), second)
            out = pl.ds(pl.multiple_of(n * 64, 64), 64)
            a_out[i, out, 0:128] = encode(total[0])
            a_out[i, out, 128:256] = encode(total[1])

        for o in offsets:
            a_copy(i, o).start()

        a_in[i, chip] = a_out[i, pl.ds(pl.multiple_of(chip * per, per), per)]

    def scan(i):
        a_all(i).wait_recv()
        carry = (jnp.zeros((per, 128), F32), jnp.zeros((per, 128), F32))
        for k in range(chips):
            c_out[i, k, :, 0:128] = encode(carry[0])
            c_out[i, k, :, 128:256] = encode(carry[1])
            if k < chips - 1:
                got = (decode(a_in[i, k, :, 0:128]), decode(a_in[i, k, :, 128:256]))
                carry = plus(times(lam2, carry), got)

        for o in offsets:
            c_copy(i, o).start()

        c_in[i, pl.ds(pl.multiple_of(chip * per, per), per)] = c_out[i, chip]

    def mate_copy(i):
        rows = pl.ds(1 + base(core, i), 2)
        return remote(st_oth.at[i], st.at[rows], s_s.at[i], s_r.at[i], mate, z)

    def mate_landed(i):
        rows = pl.ds(1 + base(1 - core, i), 2)
        return remote(st.at[rows], st.at[rows], s_s.at[i], s_r.at[i], mate, z)

    def states(i):
        c_all(i).wait_recv()
        row = base(core, i)

        @pl.loop(0, 4)
        def _(n):
            r, q = n // 2, lax.rem(n, 2)
            sub = pl.ds(pl.multiple_of(q * 64, 64), 64)
            first, second = both_feeds(i, row, r, sub)
            took = pl.ds(pl.multiple_of(n * 64, 64), 64)
            carry = (decode(c_in[i, took, 0:128]), decode(c_in[i, took, 128:256]))
            s0 = plus(times(lam, carry), first)
            s1 = plus(times(lam, s0), second)
            for p in range(2):
                lanes = slice(128 * p, 128 * p + 128)
                own = jnp.where(core == 0, s0[p], s1[p]) * (1.0 / SCALE)
                oth = jnp.where(core == 0, s1[p], s0[p]) * (1.0 / SCALE)
                st[1 + row + r, sub, lanes] = own.astype(BF16)
                st_oth[i, r, sub, lanes] = oth.astype(BF16)

        mate_copy(i).start()

    def spread_states(half, i):
        row = base(half, i)

        @pl.loop(0, 2)
        def _(r):
            spread(st[1 + row + r], 1 + row + r)

    def gelu(mixed):
        return 0.5 * mixed * (1.0 + lax.erf(mixed * (0.5 ** 0.5)))

    def finish(row):
        out = gelu(conv(w2, row)).reshape(2, 128, 256)
        ov[pl.ds(row, 2)] = (xs[pl.ds(row, 2)].astype(F32) + out).astype(BF16)

    def finish_edges():
        out = gelu(conv(w2, 0, 15)).reshape(2, 128, 256)
        ov[0] = (xs[0].astype(F32) + out[0]).astype(BF16)
        ov[15] = (xs[15].astype(F32) + out[1]).astype(BF16)

    up = remote(xs.at[0], halo.at[1], hx_s.at[0], hx_r.at[1], t, z - 1)
    down = remote(xs.at[15], halo.at[0], hx_s.at[1], hx_r.at[0], t, z + 1)
    from_up = remote(halo.at[0], halo.at[0], hx_s.at[1], hx_r.at[0], t, z - 1)
    from_down = remote(halo.at[1], halo.at[1], hx_s.at[0], hx_r.at[1], t, z + 1)

    def meet():
        pl.semaphore_wait(
            barrier,
            chips + low.astype(jnp.int32) + high.astype(jnp.int32)
            + jnp.where(core == 0, low.astype(jnp.int32), high.astype(jnp.int32)),
        )

        @pl.when(low)
        def _():
            up.start()

        @pl.when(high)
        def _():
            down.start()

    def nothing():
        pass

    load_x.wait()

    @pl.loop(0, 8)
    def _(n):
        r = jnp.where(n < 4, 1 + n, 7 + n)
        spread(xs[r], 1 + r)

    load_1.wait()
    drive(0, meet)

    @pl.loop(0, 8)
    def _(n):
        r = lax.rem(jnp.where(n < 6, 5 + n, 9 + n), 16)
        spread(xs[r], 1 + r)

    drive(1, nothing)
    aggregate(0)

    def edges(first, second):
        @pl.when(low)
        def _():
            first()

        @pl.when(jnp.logical_not(low))
        def _():
            taps[0] = jnp.zeros((128, 768), BF16)

        @pl.when(high)
        def _():
            second()

        @pl.when(jnp.logical_not(high))
        def _():
            taps[17] = jnp.zeros((128, 768), BF16)

    def halo_first():
        from_up.wait_recv()
        spread(halo[0], 0)

    def halo_second():
        from_down.wait_recv()
        spread(halo[1], 17)

    edges(halo_first, halo_second)
    drive(2, nothing)
    aggregate(1)
    drive(3, nothing)
    aggregate(2)
    aggregate(3)

    @pl.loop(0, NC)
    def _(i):
        scan(i)

    own_up = remote(st.at[1], st.at[17], hs_s.at[0], hs_r.at[1], t, z - 1)
    oth_up = remote(st_oth.at[2, 0], st.at[17], hs_s.at[1], hs_r.at[1], mate, z - 1)
    own_down = remote(st.at[16], st.at[0], hs_s.at[0], hs_r.at[0], t, z + 1)
    oth_down = remote(st_oth.at[2, 1], st.at[0], hs_s.at[1], hs_r.at[0], mate, z + 1)
    state_up = remote(st.at[0], st.at[0], hs_s.at[0], hs_r.at[0], t, z - 1)
    state_down = remote(st.at[17], st.at[17], hs_s.at[0], hs_r.at[1], t, z + 1)
    sends_up = jnp.logical_and(core == 0, low)
    sends_down = jnp.logical_and(core == 1, high)

    def inner(half, row):
        return jnp.where(half == 0, row, 14 - row)

    def state_first():
        state_up.wait_recv()
        spread(st[0], 0)

    def state_second():
        state_down.wait_recv()
        spread(st[17], 17)

    load_2.wait()
    states(0)
    spread_states(core, 0)
    states(1)
    spread_states(core, 1)
    finish(inner(core, 3))
    mate_landed(0).wait_recv()
    spread_states(1 - core, 0)
    states(2)

    @pl.when(sends_up)
    def _():
        own_up.start()
        oth_up.start()

    @pl.when(sends_down)
    def _():
        own_down.start()
        oth_down.start()

    spread_states(core, 2)
    mate_landed(1).wait_recv()
    spread_states(1 - core, 1)
    finish(inner(1 - core, 3))
    finish(inner(core, 1))
    states(3)
    spread_states(core, 3)
    finish(inner(core, 5))
    mate_landed(2).wait_recv()
    spread_states(1 - core, 2)
    finish(inner(1 - core, 1))
    mate_landed(3).wait_recv()
    spread_states(1 - core, 3)
    finish(7)
    finish(inner(1 - core, 5))
    edges(state_first, state_second)
    finish_edges()

    @pl.when(low)
    def _():
        up.wait_send()

    @pl.when(high)
    def _():
        down.wait_send()

    @pl.when(sends_up)
    def _():
        own_up.wait_send()
        oth_up.wait_send()

    @pl.when(sends_down)
    def _():
        own_down.wait_send()
        oth_down.wait_send()

    @pl.loop(0, NC)
    def _(i):
        feed_copy(i).wait_send()
        mate_copy(i).wait_send()
        a_all(i).wait_send()
        c_all(i).wait_send()


def solution(mesh):
    chips, nz = mesh.shape["tm"] // 2, mesh.shape["space"]
    per = 256 // chips
    hbm_spec = pl.BlockSpec(memory_space=pltpu.HBM)
    vmem_spec = pl.BlockSpec(memory_space=pltpu.VMEM)
    dma = pltpu.SemaphoreType.DMA

    def on_device(frames_in, w_input, decay_rate, phase, w_output):
        out = pl.pallas_call(
            functools.partial(kernel, chips, nz),
            out_shape=pltpu.VMEM((16, 128, 256), BF16),
            in_specs=[hbm_spec] * 5,
            out_specs=vmem_spec,
            scratch_shapes=[
                pltpu.VMEM((16, 128, 256), BF16),
                pltpu.VMEM((3, 768, 256), BF16),
                pltpu.VMEM((3, 768, 256), BF16),
                pltpu.VMEM((2, 1, 128), F32),
                pltpu.VMEM((2, 128, 256), BF16),
                pltpu.VMEM((18, 128, 768), BF16),
                pltpu.VMEM((16, 128, 256), F32),
                pltpu.VMEM((NC, 2, 128, 256), F32),
                pltpu.VMEM((NC, 256, 256), BF16),
                pltpu.VMEM((NC, chips, per, 256), BF16),
                pltpu.VMEM((NC, chips, per, 256), BF16),
                pltpu.VMEM((NC, 256, 256), BF16),
                pltpu.VMEM((18, 128, 256), BF16),
                pltpu.VMEM((NC, 2, 128, 256), BF16),
                dma((5,)), dma((2,)), dma((2,)), dma((NC,)), dma((NC,)),
                dma((NC,)), dma((NC,)), dma((NC,)), dma((NC,)),
                dma((NC,)), dma((NC,)), dma((2,)), dma((2,)),
            ],
            compiler_params=pltpu.CompilerParams(
                collective_id=0, has_side_effects=True, vmem_limit_bytes=40 * 1024 * 1024
            ),
            name="convs5",
        )(
            *(pltpu.with_memory_space_constraint(v, pltpu.HBM) for v in (
            frames_in[0], w_input.reshape(3, 768, 256), w_output.reshape(3, 768, 256),
            decay_rate.reshape(1, 128), phase.reshape(1, 128)))
        )
        return out[None]

    in_specs = (P("tm", "space", None, None), P(), P(), P(), P())
    return jax.shard_map(
        on_device, mesh=mesh, in_specs=in_specs,
        out_specs=P("tm", "space", None, None), check_vma=False,
    )
```

time: 40.6 us -> 31.5 us (0.78)
  local copies, waits for them, and re-layouts: 6.05 us -> 0.97 us
  Pallas kernels: 34.3 us -> 30.4 us
    unnamed x11 -> x1, local copies, waits for them, and re-layouts: 6.05 us -> 0.97 us
    pallas_call x1, Pallas kernels: 34.3 us -> 30.4 us  [on_device(): pl.pallas_call(functools.partial(kernel, chips, nz), out_shape=pltpu.VMEM...]
where the time goes in v2:
time: 31.5 us; the launch traced here: 31.4 us
  Pallas kernels  30.4 us (97%)
  local copies, waits for them, and re-layouts  0.97 us (3%)
    pallas_call x1, Pallas kernels, on_device(): pl.pallas_call(functools.partial(kernel, chips, nz), out_shape=pltpu.VMEM...  30.4 us
    unnamed x1, local copies, waits for them, and re-layouts  0.97 us

profile of v2, /device:TPU:65, one launch (start us, length us, event | category | flops | bytes accessed | tf_op | source)
XLA Modules:
  0.0 31.4 jit_solution(15212245384874842799)
XLA Ops:
  0.0 30.4 %convs5.1 = bf16[16,128,256]{2,1,0:T(8,128)(2,1)S(1)} custom-call(bf16[16,128,256]{2,1,0:T(8,128)(2,1)} %bitcast.9, bf16[3,768,256]{2,1,0:T(8,128)(2,1)} %bitcast.7, bf16[3,768,256]{2,1,0:T(8,128)(2,1)} %bitcast.8, f32[1,128]{1,0:T(1,128)} %bitcast.10, f32[1,128]{1,0:T(1,128)} %bitcast.11), custom_call_target="tpu_custom_call" | custom-call | tf_op jit(solution)/shard_map/convs5/pallas_call | solution.py:430
  30.4 1.0 %copy.7 = bf16[1,16,128,256]{3,2,1,0:T(8,128)(2,1)} copy(bf16[1,16,128,256]{3,2,1,0:T(8,128)(2,1)S(1)} %bitcast.6) | data formatting | bytes 2097152

commit v3 on v2

--- a/solution.py
+++ b/solution.py
@@ -10,6 +10,7 @@
 MESH = pl.DeviceIdType.MESH
 NC = 4
 SCALE = 16384.0
+TINY = 1.2e-38
 F32 = jnp.float32
 BF16 = jnp.bfloat16
 
@@ -20,7 +21,9 @@
 
 def decode(code):
     w = code.astype(F32)
-    root = jnp.sqrt(jnp.sqrt(jnp.abs(w)))
+    size = jnp.abs(w)
+    half = size * lax.rsqrt(jnp.maximum(size, TINY))
+    root = half * lax.rsqrt(jnp.maximum(half, TINY))
     return jnp.where(w < 0, -root, root)
 
 
@@ -87,16 +90,28 @@
     for o in offsets:
         greet(2 * peer(o) + core, z)
 
-    load_x = pltpu.make_async_copy(x_hbm, xs, ld_sem.at[0])
-    load_1 = pltpu.make_async_copy(w1_hbm, w1, ld_sem.at[1])
+
+    def load_rows(first, count, sem):
+        rows = pl.ds(first, count)
+        return pltpu.make_async_copy(x_hbm.at[rows], xs.at[rows], ld_sem.at[sem])
+
+    load_a, load_b = load_rows(1, 4, 0), load_rows(11, 4, 5)
+    load_rest = (load_rows(0, 1, 6), load_rows(15, 1, 7), load_rows(5, 6, 8))
+    load_1 = [
+        pltpu.make_async_copy(w1_hbm.at[dy], w1.at[dy], ld_sem.at[sem])
+        for dy, sem in enumerate((1, 9, 10))
+    ]
     load_2 = pltpu.make_async_copy(w2_hbm, w2, ld_sem.at[2])
     load_d = pltpu.make_async_copy(decay_hbm, rates.at[0], ld_sem.at[3])
     load_p = pltpu.make_async_copy(phase_hbm, rates.at[1], ld_sem.at[4])
-    load_x.start()
+    load_a.start()
+    load_b.start()
+    for copy in load_1:
+        copy.start()
     load_d.start()
     load_p.start()
-    load_1.start()
-    load_2.start()
+    for copy in load_rest:
+        copy.start()
 
     load_d.wait()
     load_p.wait()
@@ -120,9 +135,11 @@
         taps[slot, :, 256:512] = row
         taps[slot, :, 512:768] = right.astype(BF16)
 
-    def conv(w, row, other=None):
+    def conv(w, row, other=None, loads=None):
         acc = None
         for dy in range(3):
+            if loads is not None:
+                loads[dy].wait()
             if other is None:
                 seen = taps[pl.ds(row + dy, 2)].reshape(256, 768)
             else:
@@ -131,42 +148,35 @@
             acc = part if acc is None else acc + part
         return acc
 
-    def drive(i, between):
-        @pl.loop(0, 2)
-        def _(n):
-            row = base(jnp.where(n == 0, 1 - core, core), i)
-            f_own[pl.ds(row, 2)] = (conv(w1, row) * factor).reshape(2, 128, 256)
-
-            @pl.when(n == 0)
-            def _():
-                between()
-                feed_copy(i).start()
+    def drive(half, i, loads=None):
+        row = base(half, i)
+        f_own[pl.ds(row, 2)] = (conv(w1, row, loads=loads) * factor).reshape(2, 128, 256)
 
     def feed_copy(i):
         rows = pl.ds(base(1 - core, i), 2)
-        return remote(f_own.at[rows], f_par.at[i], f_s.at[i], f_r.at[i], mate, z)
+        return remote(f_own.at[rows], f_par.at[i], f_s.at[0], f_r.at[i], mate, z)
 
     def a_copy(i, d):
         j = peer(d)
         return remote(
             a_out.at[i, pl.ds(pl.multiple_of(j * per, per), per)], a_in.at[i, chip],
-            a_s.at[i], a_r.at[i], 2 * j + core, z,
+            a_s.at[0], a_r.at[i], 2 * j + core, z,
         )
 
     def a_all(i):
         blocks = a_in.at[i, pl.ds(0, chips - 1)]
-        return remote(blocks, blocks, a_s.at[i], a_r.at[i], mate, z)
+        return remote(blocks, blocks, a_s.at[0], a_r.at[i], mate, z)
 
     def c_copy(i, d):
         j = peer(d)
         return remote(
             c_out.at[i, j], c_in.at[i, pl.ds(pl.multiple_of(chip * per, per), per)],
-            c_s.at[i], c_r.at[i], 2 * j + core, z,
+            c_s.at[0], c_r.at[i], 2 * j + core, z,
         )
 
     def c_all(i):
         blocks = c_in.at[i, pl.ds(0, (chips - 1) * per)]
-        return remote(blocks, blocks, c_s.at[i], c_r.at[i], mate, z)
+        return remote(blocks, blocks, c_s.at[0], c_r.at[i], mate, z)
 
     def both_feeds(i, row, r, sub):
         mine = f_own[row + r, sub]
@@ -211,11 +221,11 @@
 
     def mate_copy(i):
         rows = pl.ds(1 + base(core, i), 2)
-        return remote(st_oth.at[i], st.at[rows], s_s.at[i], s_r.at[i], mate, z)
+        return remote(st_oth.at[i], st.at[rows], s_s.at[0], s_r.at[i], mate, z)
 
     def mate_landed(i):
         rows = pl.ds(1 + base(1 - core, i), 2)
-        return remote(st.at[rows], st.at[rows], s_s.at[i], s_r.at[i], mate, z)
+        return remote(st.at[rows], st.at[rows], s_s.at[0], s_r.at[i], mate, z)
 
     def states(i):
         c_all(i).wait_recv()
@@ -278,61 +288,76 @@
         def _():
             down.start()
 
-    def nothing():
-        pass
-
-    load_x.wait()
+    load_a.wait()
+    load_b.wait()
+
+    def edges(first, second):
+        @pl.when(low)
+        def _():
+            first()
+
+        @pl.when(jnp.logical_not(low))
+        def _():
+            taps[0] = jnp.zeros((128, 768), BF16)
+
+        @pl.when(high)
+        def _():
+            second()
+
+        @pl.when(jnp.logical_not(high))
+        def _():
+            taps[17] = jnp.zeros((128, 768), BF16)
+
+    def halo_first():
+        from_up.wait_recv()
+        spread(halo[0], 0)
+
+    def halo_second():
+        from_down.wait_recv()
+        spread(halo[1], 17)
+
+    mate_half = 1 - core
 
     @pl.loop(0, 8)
     def _(n):
         r = jnp.where(n < 4, 1 + n, 7 + n)
         spread(xs[r], 1 + r)
 
-    load_1.wait()
-    drive(0, meet)
-
-    @pl.loop(0, 8)
+    drive(mate_half, 0, load_1)
+    load_2.start()
+    for copy in load_rest:
+        copy.wait()
+    meet()
+    feed_copy(0).start()
+    drive(core, 0)
+
+    @pl.loop(0, 4)
     def _(n):
-        r = lax.rem(jnp.where(n < 6, 5 + n, 9 + n), 16)
+        r = jnp.where(n < 2, 5 + n, 7 + n)
         spread(xs[r], 1 + r)
 
-    drive(1, nothing)
+    drive(mate_half, 1)
+    feed_copy(1).start()
     aggregate(0)
 
-    def edges(first, second):
-        @pl.when(low)
-        def _():
-            first()
-
-        @pl.when(jnp.logical_not(low))
-        def _():
-            taps[0] = jnp.zeros((128, 768), BF16)
-
-        @pl.when(high)
-        def _():
-            second()
-
-        @pl.when(jnp.logical_not(high))
-        def _():
-            taps[17] = jnp.zeros((128, 768), BF16)
-
-    def halo_first():
-        from_up.wait_recv()
-        spread(halo[0], 0)
-
-    def halo_second():
-        from_down.wait_recv()
-        spread(halo[1], 17)
-
+    @pl.loop(0, 4)
+    def _(n):
+        r = jnp.where(n < 2, 7 + n, 15 * (n - 2))
+        spread(xs[r], 1 + r)
+
+    drive(core, 1)
+    drive(mate_half, 3)
+    feed_copy(3).start()
+    aggregate(1)
+    drive(core, 3)
     edges(halo_first, halo_second)
-    drive(2, nothing)
-    aggregate(1)
-    drive(3, nothing)
+    drive(mate_half, 2)
+    feed_copy(2).start()
+    aggregate(3)
+    drive(core, 2)
     aggregate(2)
-    aggregate(3)
-
-    @pl.loop(0, NC)
-    def _(i):
+
+    for i in (0, 1, 3, 2):
         scan(i)
 
     own_up = remote(st.at[1], st.at[17], hs_s.at[0], hs_r.at[1], t, z - 1)
@@ -363,6 +388,12 @@
     finish(inner(core, 3))
     mate_landed(0).wait_recv()
     spread_states(1 - core, 0)
+    states(3)
+    spread_states(core, 3)
+    mate_landed(1).wait_recv()
+    spread_states(1 - core, 1)
+    finish(inner(core, 5))
+    finish(inner(1 - core, 3))
     states(2)
 
     @pl.when(sends_up)
@@ -376,20 +407,14 @@
         oth_down.start()
 
     spread_states(core, 2)
-    mate_landed(1).wait_recv()
-    spread_states(1 - core, 1)
-    finish(inner(1 - core, 3))
-    finish(inner(core, 1))
-    states(3)
-    spread_states(core, 3)
-    finish(inner(core, 5))
-    mate_landed(2).wait_recv()
-    spread_states(1 - core, 2)
-    finish(inner(1 - core, 1))
     mate_landed(3).wait_recv()
     spread_states(1 - core, 3)
     finish(7)
     finish(inner(1 - core, 5))
+    finish(inner(core, 1))
+    mate_landed(2).wait_recv()
+    spread_states(1 - core, 2)
+    finish(inner(1 - core, 1))
     edges(state_first, state_second)
     finish_edges()
 
@@ -411,12 +436,11 @@
         own_down.wait_send()
         oth_down.wait_send()
 
-    @pl.loop(0, NC)
-    def _(i):
-        feed_copy(i).wait_send()
-        mate_copy(i).wait_send()
-        a_all(i).wait_send()
-        c_all(i).wait_send()
+    blocks = a_in.at[:, pl.ds(0, chips - 1)]
+    remote(f_par, f_par, f_s.at[0], f_r.at[0], mate, z).wait_send()
+    remote(st_oth, st_oth, s_s.at[0], s_r.at[0], mate, z).wait_send()
+    remote(blocks, blocks, a_s.at[0], a_r.at[0], mate, z).wait_send()
+    remote(blocks, blocks, c_s.at[0], c_r.at[0], mate, z).wait_send()
 
 
 def solution(mesh):
@@ -447,9 +471,9 @@
                 pltpu.VMEM((NC, 256, 256), BF16),
                 pltpu.VMEM((18, 128, 256), BF16),
                 pltpu.VMEM((NC, 2, 128, 256), BF16),
-                dma((5,)), dma((2,)), dma((2,)), dma((NC,)), dma((NC,)),
-                dma((NC,)), dma((NC,)), dma((NC,)), dma((NC,)),
-                dma((NC,)), dma((NC,)), dma((2,)), dma((2,)),
+                dma((11,)), dma((2,)), dma((2,)), dma((1,)), dma((NC,)),
+                dma((1,)), dma((NC,)), dma((1,)), dma((NC,)),
+                dma((1,)), dma((NC,)), dma((2,)), dma((2,)),
             ],
             compiler_params=pltpu.CompilerParams(
                 collective_id=0, has_side_effects=True, vmem_limit_bytes=40 * 1024 * 1024

time: 31.5 us -> 30.5 us (0.968)
  Pallas kernels: 30.4 us -> 29.4 us
    pallas_call x1, Pallas kernels: 30.4 us -> 29.4 us  [on_device(): pl.pallas_call(functools.partial(kernel, chips, nz), out_shape=pltpu.VMEM...]
where the time goes in v3:
time: 30.5 us; the launch traced here: 30.4 us
  Pallas kernels  29.4 us (96%)
  local copies, waits for them, and re-layouts  0.97 us (3%)
    pallas_call x1, Pallas kernels, on_device(): pl.pallas_call(functools.partial(kernel, chips, nz), out_shape=pltpu.VMEM...  29.4 us
    unnamed x1, local copies, waits for them, and re-layouts  0.97 us

profile of v3, /device:TPU:65, one launch (start us, length us, event | category | flops | bytes accessed | tf_op | source)
XLA Modules:
  0.0 30.4 jit_solution(15954813019922446869)
XLA Ops:
  0.0 29.4 %convs5.1 = bf16[16,128,256]{2,1,0:T(8,128)(2,1)S(1)} custom-call(bf16[16,128,256]{2,1,0:T(8,128)(2,1)} %bitcast.9, bf16[3,768,256]{2,1,0:T(8,128)(2,1)} %bitcast.7, bf16[3,768,256]{2,1,0:T(8,128)(2,1)} %bitcast.8, f32[1,128]{1,0:T(1,128)} %bitcast.10, f32[1,128]{1,0:T(1,128)} %bitcast.11), custom_call_target="tpu_custom_call" | custom-call | tf_op jit(solution)/shard_map/convs5/pallas_call | solution.py:454
  29.5 1.0 %copy.7 = bf16[1,16,128,256]{3,2,1,0:T(8,128)(2,1)} copy(bf16[1,16,128,256]{3,2,1,0:T(8,128)(2,1)S(1)} %bitcast.6) | data formatting | bytes 2097152

commit v4 on v3

--- a/solution.py
+++ b/solution.py
@@ -39,7 +39,7 @@
     chips, nz,
     x_hbm, w1_hbm, w2_hbm, decay_hbm, phase_hbm,
     ov,
-    xs, w1, w2, rates, halo, taps, f_own, f_par, a_out, a_in, c_out, c_in, st, st_oth,
+    xs, w1, w2, rates, halo, taps, f_own, f_par, a_out, a_in, c_out, c_in, st, st_oth, part,
     ld_sem, hx_s, hx_r, f_s, f_r, a_s, a_r, c_s, c_r, s_s, s_r, hs_s, hs_r,
 ):
     t, z = lax.axis_index("tm"), lax.axis_index("space")
@@ -69,26 +69,25 @@
     def greet(tm, zz):
         pl.semaphore_signal(barrier, inc=1, device_id=(tm, zz), device_id_type=MESH)
 
-    greet(mate, z)
-
-    @pl.when(low)
-    def _():
-        greet(t, z - 1)
-
-    @pl.when(high)
-    def _():
-        greet(t, z + 1)
-
-    @pl.when(jnp.logical_and(low, core == 0))
-    def _():
-        greet(mate, z - 1)
-
-    @pl.when(jnp.logical_and(high, core == 1))
-    def _():
-        greet(mate, z + 1)
-
     for o in offsets:
         greet(2 * peer(o) + core, z)
+    greet(mate, z)
+
+    @pl.when(low)
+    def _():
+        greet(t, z - 1)
+
+    @pl.when(high)
+    def _():
+        greet(t, z + 1)
+
+    @pl.when(jnp.logical_and(low, core == 0))
+    def _():
+        greet(mate, z - 1)
+
+    @pl.when(jnp.logical_and(high, core == 1))
+    def _():
+        greet(mate, z + 1)
 
 
     def load_rows(first, count, sem):
@@ -227,12 +226,13 @@
         rows = pl.ds(1 + base(1 - core, i), 2)
         return remote(st.at[rows], st.at[rows], s_s.at[0], s_r.at[i], mate, z)
 
-    def states(i):
+    def states(i, after_edge=None):
         c_all(i).wait_recv()
         row = base(core, i)
 
         @pl.loop(0, 4)
-        def _(n):
+        def _(step):
+            n = step if after_edge is None else lax.rem(step + 2 * core, 4)
             r, q = n // 2, lax.rem(n, 2)
             sub = pl.ds(pl.multiple_of(q * 64, 64), 64)
             first, second = both_feeds(i, row, r, sub)
@@ -247,6 +247,9 @@
                 st[1 + row + r, sub, lanes] = own.astype(BF16)
                 st_oth[i, r, sub, lanes] = oth.astype(BF16)
 
+            if after_edge is not None:
+                pl.when(step == 1)(after_edge)
+
         mate_copy(i).start()
 
     def spread_states(half, i):
@@ -263,10 +266,18 @@
         out = gelu(conv(w2, row)).reshape(2, 128, 256)
         ov[pl.ds(row, 2)] = (xs[pl.ds(row, 2)].astype(F32) + out).astype(BF16)
 
+    def start_edges():
+        for n, (row, taken) in enumerate(((0, (1, 2)), (15, (0, 1)))):
+            acc = None
+            for dy in taken:
+                more = jnp.dot(taps[row + dy], w2[dy], preferred_element_type=F32)
+                acc = more if acc is None else acc + more
+            part[n] = acc
+
     def finish_edges():
-        out = gelu(conv(w2, 0, 15)).reshape(2, 128, 256)
-        ov[0] = (xs[0].astype(F32) + out[0]).astype(BF16)
-        ov[15] = (xs[15].astype(F32) + out[1]).astype(BF16)
+        for n, (row, dy) in enumerate(((0, 0), (15, 2))):
+            mixed = part[n] + jnp.dot(taps[row + dy], w2[dy], preferred_element_type=F32)
+            ov[row] = (xs[row].astype(F32) + gelu(mixed)).astype(BF16)
 
     up = remote(xs.at[0], halo.at[1], hx_s.at[0], hx_r.at[1], t, z - 1)
     down = remote(xs.at[15], halo.at[0], hx_s.at[1], hx_r.at[0], t, z + 1)
@@ -371,6 +382,17 @@
 
     def inner(half, row):
         return jnp.where(half == 0, row, 14 - row)
+
+    def send_edges():
+        @pl.when(sends_up)
+        def _():
+            own_up.start()
+            oth_up.start()
+
+        @pl.when(sends_down)
+        def _():
+            own_down.start()
+            oth_down.start()
 
     def state_first():
         state_up.wait_recv()
@@ -394,18 +416,7 @@
     spread_states(1 - core, 1)
     finish(inner(core, 5))
     finish(inner(1 - core, 3))
-    states(2)
-
-    @pl.when(sends_up)
-    def _():
-        own_up.start()
-        oth_up.start()
-
-    @pl.when(sends_down)
-    def _():
-        own_down.start()
-        oth_down.start()
-
+    states(2, send_edges)
     spread_states(core, 2)
     mate_landed(3).wait_recv()
     spread_states(1 - core, 3)
@@ -415,6 +426,7 @@
     mate_landed(2).wait_recv()
     spread_states(1 - core, 2)
     finish(inner(1 - core, 1))
+    start_edges()
     edges(state_first, state_second)
     finish_edges()
 
@@ -471,6 +483,7 @@
                 pltpu.VMEM((NC, 256, 256), BF16),
                 pltpu.VMEM((18, 128, 256), BF16),
                 pltpu.VMEM((NC, 2, 128, 256), BF16),
+                pltpu.VMEM((2, 128, 256), F32),
                 dma((11,)), dma((2,)), dma((2,)), dma((1,)), dma((NC,)),
                 dma((1,)), dma((NC,)), dma((1,)), dma((NC,)),
                 dma((1,)), dma((NC,)), dma((2,)), dma((2,)),

time: 30.5 us -> 30 us (0.984)
  Pallas kernels: 29.4 us -> 29 us
    pallas_call x1, Pallas kernels: 29.4 us -> 29 us  [on_device(): pl.pallas_call(functools.partial(kernel, chips, nz), out_shape=pltpu.VMEM...]
where the time goes in v4:
time: 30 us; the launch traced here: 29.9 us
  Pallas kernels  29 us (97%)
  local copies, waits for them, and re-layouts  0.97 us (3%)
    pallas_call x1, Pallas kernels, on_device(): pl.pallas_call(functools.partial(kernel, chips, nz), out_shape=pltpu.VMEM...  29 us
    unnamed x1, local copies, waits for them, and re-layouts  0.97 us

profile of v4, /device:TPU:65, one launch (start us, length us, event | category | flops | bytes accessed | tf_op | source)
XLA Modules:
  0.0 29.9 jit_solution(13368218821958347981)
XLA Ops:
  0.0 29.0 %convs5.1 = bf16[16,128,256]{2,1,0:T(8,128)(2,1)S(1)} custom-call(bf16[16,128,256]{2,1,0:T(8,128)(2,1)} %bitcast.9, bf16[3,768,256]{2,1,0:T(8,128)(2,1)} %bitcast.7, bf16[3,768,256]{2,1,0:T(8,128)(2,1)} %bitcast.8, f32[1,128]{1,0:T(1,128)} %bitcast.10, f32[1,128]{1,0:T(1,128)} %bitcast.11), custom_call_target="tpu_custom_call" | custom-call | tf_op jit(solution)/shard_map/convs5/pallas_call | solution.py:466
  29.0 1.0 %copy.7 = bf16[1,16,128,256]{3,2,1,0:T(8,128)(2,1)} copy(bf16[1,16,128,256]{3,2,1,0:T(8,128)(2,1)S(1)} %bitcast.6) | data formatting | bytes 2097152

commit v5 on v4

--- a/solution.py
+++ b/solution.py
@@ -338,14 +338,15 @@
     load_2.start()
     for copy in load_rest:
         copy.wait()
-    meet()
-    feed_copy(0).start()
-    drive(core, 0)
 
     @pl.loop(0, 4)
     def _(n):
         r = jnp.where(n < 2, 5 + n, 7 + n)
         spread(xs[r], 1 + r)
+
+    meet()
+    feed_copy(0).start()
+    drive(core, 0)
 
     drive(mate_half, 1)
     feed_copy(1).start()
@@ -418,11 +419,11 @@
     finish(inner(1 - core, 3))
     states(2, send_edges)
     spread_states(core, 2)
+    finish(inner(core, 1))
     mate_landed(3).wait_recv()
     spread_states(1 - core, 3)
     finish(7)
     finish(inner(1 - core, 5))
-    finish(inner(core, 1))
     mate_landed(2).wait_recv()
     spread_states(1 - core, 2)
     finish(inner(1 - core, 1))

time: 30 us -> 30.1 us (level)
  no operation moved by 1% of the time
where the time goes in v5:
time: 30.1 us; the launch traced here: 30 us
  Pallas kernels  29 us (96%)
  local copies, waits for them, and re-layouts  0.97 us (3%)
    pallas_call x1, Pallas kernels, on_device(): pl.pallas_call(functools.partial(kernel, chips, nz), out_shape=pltpu.VMEM...  29 us
    unnamed x1, local copies, waits for them, and re-layouts  0.97 us

profile of v5, /device:TPU:65, one launch (start us, length us, event | category | flops | bytes accessed | tf_op | source)
XLA Modules:
  0.0 30.0 jit_solution(12904667857090812839)
XLA Ops:
  0.0 29.0 %convs5.1 = bf16[16,128,256]{2,1,0:T(8,128)(2,1)S(1)} custom-call(bf16[16,128,256]{2,1,0:T(8,128)(2,1)} %bitcast.9, bf16[3,768,256]{2,1,0:T(8,128)(2,1)} %bitcast.7, bf16[3,768,256]{2,1,0:T(8,128)(2,1)} %bitcast.8, f32[1,128]{1,0:T(1,128)} %bitcast.10, f32[1,128]{1,0:T(1,128)} %bitcast.11), custom_call_target="tpu_custom_call" | custom-call | tf_op jit(solution)/shard_map/convs5/pallas_call | solution.py:467
  29.1 1.0 %copy.7 = bf16[1,16,128,256]{3,2,1,0:T(8,128)(2,1)} copy(bf16[1,16,128,256]{3,2,1,0:T(8,128)(2,1)S(1)} %bitcast.6) | data formatting | bytes 2097152
